TPU v7x, 32 devices: a whole 2x2x4 slice. The times are simulated.
32 devices in a mesh: dp: 16 (over z, x, core), tensor: 2 (over y).
Axes of the slice: x: 2, y: 2, z: 4, core: 2. Of those that a mesh axis runs over, the one named last changes fastest.
Arguments:
- tokens: bfloat16 [32768, 768], P(('dp', 'tensor')), may hold values from -6 to 6
- segment_ids: int32 [16, 2048], P('dp'), may hold values from 0 to 15, never falling along the last dimension, each value on 1 to 1024 neighbouring positions
- ln1_gain: bfloat16 [768], P('dp'), may hold values from 0.25 to 1.75
- ln1_bias: bfloat16 [768], P('dp'), may hold values from -1.796875 to 1.796875
- w_qkv: bfloat16 [768, 3, 768], P('dp', None, 'tensor'), may hold values from -0.3125 to 0.3125
- b_qv: bfloat16 [2, 768], P(None, 'dp'), may hold values from -1.796875 to 1.796875
- w_attn_out: bfloat16 [768, 768], P('tensor', 'dp'), may hold values from -3 to 3
- b_attn_out: bfloat16 [768], P('dp'), may hold values from -6 to 6
- ln2_gain: bfloat16 [768], P('dp'), may hold values from 0.25 to 1.75
- ln2_bias: bfloat16 [768], P('dp'), may hold values from -1.796875 to 1.796875
- w_fc: bfloat16 [768, 3072], P('dp', 'tensor'), may hold values from -0.21875 to 0.21875
- b_fc: bfloat16 [3072], P('dp'), may hold values from -1.796875 to 1.796875
- w_proj: bfloat16 [3072, 768], P('tensor', 'dp'), may hold values from -0.8984375 to 0.8984375
- b_proj: bfloat16 [768], P('dp'), may hold values from -6 to 6
- cotangent: bfloat16 [32768, 768], P(('dp', 'tensor')), may hold values from -6 to 6
Outputs:
- block_out: bfloat16 [32768, 768], P(('dp', 'tensor'))
- grad_tokens: bfloat16 [32768, 768], P(('dp', 'tensor'))
- grad_ln1_gain: float32 [768], P('dp')
- grad_ln1_bias: float32 [768], P('dp')
- grad_w_qkv: float32 [768, 3, 768], P('dp', None, 'tensor')
- grad_b_qv: float32 [2, 768], P(None, 'dp')
- grad_w_attn_out: float32 [768, 768], P('tensor', 'dp')
- grad_b_attn_out: float32 [768], P('dp')
- grad_ln2_gain: float32 [768], P('dp')
- grad_ln2_bias: float32 [768], P('dp')
- grad_w_fc: float32 [768, 3072], P('dp', 'tensor')
- grad_b_fc: float32 [3072], P('dp')
- grad_w_proj: float32 [3072, 768], P('tensor', 'dp')
- grad_b_proj: float32 [768], P('dp')
Inputs may be any that keep to these rules, and one draw needn't show every extreme that they name: `segment_ids`: in each sequence the document numbers never fall; each document has 1 to 1024 tokens, and one has exactly 1024.
All inputs are finite; a program needn't handle non-finite values.
Results may differ from a plain program's by a relative error of at most 0.02.
Values may be sent and summed in bfloat16 or wider, within the bound.
A program may use at most 256 MiB of HBM per device.

v0:
```python
import jax
import jax.numpy as jnp
from jax import lax
from jax.sharding import PartitionSpec as P

HEAD_DIM = 64
EPSILON = 1e-05
BRANCH_SCALE = 48.0 ** (-0.5)
MASKED_SCORE = -1e30


def layer_norm(values, gain, offsets):
    centered = values - jnp.mean(values, axis=-1, keepdims=True)
    variance = jnp.mean(centered * centered, axis=-1, keepdims=True)
    return centered * lax.rsqrt(variance + EPSILON) * gain + offsets


def gelu_tanh(values):
    return jax.nn.gelu(values, approximate=True)


def contract_rows(left, right):
    return lax.dot_general(
        left, right, (((0,), (0,)), ((), ())), preferred_element_type=jnp.float32
    )


def contract_cols(left, right):
    return lax.dot_general(
        left, right, (((1,), (1,)), ((), ())), preferred_element_type=jnp.float32
    )


def visible_mask(seg_row, row_start, block_rows):
    seq_len = seg_row.shape[0]
    seg_query = lax.dynamic_slice_in_dim(seg_row, row_start, block_rows, 0)
    query_pos = row_start + jnp.arange(block_rows, dtype=jnp.int32)
    key_pos = jnp.arange(seq_len, dtype=jnp.int32)
    return (seg_query[:, None] == seg_row[None, :]) & (query_pos[:, None] >= key_pos[None, :])


def on_device(
    tokens,
    segment_ids,
    ln1_gain,
    ln1_bias,
    w_qkv,
    b_qv,
    w_attn_out,
    b_attn_out,
    ln2_gain,
    ln2_bias,
    w_fc,
    b_fc,
    w_proj,
    b_proj,
    cotangent,
):
    model_width = tokens.shape[1]
    local_rows = tokens.shape[0]
    local_cols = w_qkv.shape[2]
    hidden_cols = w_fc.shape[1]
    heads_here = local_cols // HEAD_DIM
    seg_row = segment_ids[0]
    seq_len = seg_row.shape[0]
    score_scale = HEAD_DIM ** (-0.5)
    tensor_pos = lax.axis_index("tensor")
    gain_attn, offset_attn, qkv_weight, qv_bias_all, out_weight, out_bias = (
        lax.all_gather(ln1_gain, "dp", axis=0, tiled=True),
        lax.all_gather(ln1_bias, "dp", axis=0, tiled=True),
        lax.all_gather(w_qkv, "dp", axis=0, tiled=True),
        lax.all_gather(b_qv, "dp", axis=1, tiled=True),
        lax.all_gather(w_attn_out, "dp", axis=1, tiled=True),
        lax.all_gather(b_attn_out, "dp", axis=0, tiled=True),
    )
    qkv_flat_weight = qkv_weight.reshape(model_width, 3 * local_cols)
    qv_bias = lax.dynamic_slice_in_dim(qv_bias_all, tensor_pos * local_cols, local_cols, 1).astype(
        jnp.float32
    )
    qkv_bias = jnp.stack([qv_bias[0], jnp.zeros((local_cols,), jnp.float32), qv_bias[1]])
    residual_in = tokens.astype(jnp.float32)
    normed_one = layer_norm(
        residual_in, gain_attn.astype(jnp.float32), offset_attn.astype(jnp.float32)
    ).astype(jnp.bfloat16)
    full_one = lax.all_gather(normed_one, "tensor", axis=0, tiled=True)
    projected = (
        jnp.dot(full_one, qkv_flat_weight, preferred_element_type=jnp.float32).reshape(
            seq_len, 3, local_cols
        )
        + qkv_bias
    ).astype(jnp.bfloat16)
    queries = projected[:, 0]
    keys_all = projected[:, 1]
    values_all = projected[:, 2]
    block_rows = min(512, seq_len)
    starts = jnp.arange(seq_len // block_rows, dtype=jnp.int32) * block_rows

    def forward_block(row_start):
        visible = visible_mask(seg_row, row_start, block_rows)
        query_block = lax.dynamic_slice_in_dim(queries, row_start, block_rows, 0)
        pieces = []
        logsums = []
        for head_index in range(heads_here):
            low_col = head_index * HEAD_DIM
            high_col = low_col + HEAD_DIM
            raw_scores = contract_cols(
                query_block[:, low_col:high_col], keys_all[:, low_col:high_col]
            )
            scores = jnp.where(visible, raw_scores * score_scale, MASKED_SCORE)
            row_max = jnp.max(scores, axis=1, keepdims=True)
            exponent = jnp.exp(scores - row_max)
            row_total = jnp.sum(exponent, axis=1, keepdims=True)
            soft_weights = (exponent / row_total).astype(jnp.bfloat16)
            pieces.append(
                jnp.dot(
                    soft_weights,
                    values_all[:, low_col:high_col],
                    preferred_element_type=jnp.float32,
                )
            )
            logsums.append(row_max[:, 0] + jnp.log(row_total[:, 0]))
        return (jnp.concatenate(pieces, axis=1).astype(jnp.bfloat16), jnp.stack(logsums))

    attn_blocks, logsum_blocks = lax.map(forward_block, starts)
    attended = attn_blocks.reshape(seq_len, local_cols)
    attn_branch = lax.psum_scatter(
        jnp.dot(
            lax.slice_in_dim(attended, 0, lax.axis_size("tensor") * local_rows, axis=0),
            out_weight,
            preferred_element_type=jnp.float32,
        ).astype(jnp.bfloat16),
        "tensor",
        scatter_dimension=0,
        tiled=True,
    ).astype(jnp.float32) + out_bias.astype(jnp.float32)
    middle = residual_in + BRANCH_SCALE * attn_branch
    gain_mlp, offset_mlp, fc_weight, fc_bias_all, proj_weight, proj_bias = (
        lax.all_gather(ln2_gain, "dp", axis=0, tiled=True),
        lax.all_gather(ln2_bias, "dp", axis=0, tiled=True),
        lax.all_gather(w_fc, "dp", axis=0, tiled=True),
        lax.all_gather(b_fc, "dp", axis=0, tiled=True),
        lax.all_gather(w_proj, "dp", axis=1, tiled=True),
        lax.all_gather(b_proj, "dp", axis=0, tiled=True),
    )
    fc_bias = lax.dynamic_slice_in_dim(
        fc_bias_all, tensor_pos * hidden_cols, hidden_cols, 0
    ).astype(jnp.float32)
    normed_two = layer_norm(
        middle, gain_mlp.astype(jnp.float32), offset_mlp.astype(jnp.float32)
    ).astype(jnp.bfloat16)
    full_two = lax.all_gather(normed_two, "tensor", axis=0, tiled=True)
    inputs_rows = lax.slice_in_dim(full_two, 0, lax.axis_size("tensor") * local_rows, axis=0)
    activated = gelu_tanh(
        jnp.dot(inputs_rows, fc_weight, preferred_element_type=jnp.float32) + fc_bias
    ).astype(jnp.bfloat16)
    mlp_branch = lax.psum_scatter(
        jnp.dot(activated, proj_weight, preferred_element_type=jnp.float32).astype(jnp.bfloat16),
        "tensor",
        scatter_dimension=0,
        tiled=True,
    ).astype(jnp.float32) + proj_bias.astype(jnp.float32)
    block_out = (middle + BRANCH_SCALE * mlp_branch).astype(jnp.bfloat16)
    (
        gain_attn,
        offset_attn,
        qkv_weight,
        out_weight,
        gain_mlp,
        offset_mlp,
        fc_weight,
        fc_bias_all,
        proj_weight,
    ) = (
        lax.all_gather(ln1_gain, "dp", axis=0, tiled=True),
        lax.all_gather(ln1_bias, "dp", axis=0, tiled=True),
        lax.all_gather(w_qkv, "dp", axis=0, tiled=True),
        lax.all_gather(w_attn_out, "dp", axis=1, tiled=True),
        lax.all_gather(ln2_gain, "dp", axis=0, tiled=True),
        lax.all_gather(ln2_bias, "dp", axis=0, tiled=True),
        lax.all_gather(w_fc, "dp", axis=0, tiled=True),
        lax.all_gather(b_fc, "dp", axis=0, tiled=True),
        lax.all_gather(w_proj, "dp", axis=1, tiled=True),
    )
    qkv_flat_weight = qkv_weight.reshape(model_width, 3 * local_cols)
    fc_bias = lax.dynamic_slice_in_dim(
        fc_bias_all, tensor_pos * hidden_cols, hidden_cols, 0
    ).astype(jnp.float32)
    grad_out = cotangent.astype(jnp.float32)
    scaled_out = BRANCH_SCALE * grad_out
    d_proj_bias = jnp.sum(scaled_out, axis=0)
    d_mlp_full = lax.all_gather(scaled_out.astype(jnp.bfloat16), "tensor", axis=0, tiled=True)
    mlp_block = min(1024, seq_len)

    def mlp_back_block(row_start):
        inputs_rows = lax.dynamic_slice_in_dim(full_two, row_start, mlp_block, 0)
        grad_rows = lax.dynamic_slice_in_dim(d_mlp_full, row_start, mlp_block, 0)
        pre_act = jnp.dot(inputs_rows, fc_weight, preferred_element_type=jnp.float32) + fc_bias
        activated, gelu_back = jax.vjp(gelu_tanh, pre_act)
        d_act = contract_cols(grad_rows, proj_weight)
        d_pre = gelu_back(d_act)[0]
        return (activated.astype(jnp.bfloat16), d_pre.astype(jnp.bfloat16), jnp.sum(d_pre, axis=0))

    act_blocks, dpre_blocks, dbias_blocks = lax.map(
        mlp_back_block, jnp.arange(seq_len // mlp_block, dtype=jnp.int32) * mlp_block
    )
    act_all = act_blocks.reshape(seq_len, hidden_cols)
    d_pre_all = dpre_blocks.reshape(seq_len, hidden_cols)
    d_fc_bias = jnp.sum(dbias_blocks, axis=0)
    d_proj_w = contract_rows(act_all, d_mlp_full)
    d_fc_w = contract_rows(full_two, d_pre_all)
    grad_w_fc, grad_w_proj = (
        lax.psum_scatter(d_fc_w, "dp", scatter_dimension=0, tiled=True),
        lax.psum_scatter(d_proj_w, "dp", scatter_dimension=1, tiled=True),
    )
    d_normed_two = lax.psum_scatter(
        contract_cols(
            lax.slice_in_dim(d_pre_all, 0, lax.axis_size("tensor") * local_rows, axis=0), fc_weight
        ).astype(jnp.bfloat16),
        "tensor",
        scatter_dimension=0,
        tiled=True,
    ).astype(jnp.float32)
    unused_two, norm_back_two = jax.vjp(
        layer_norm, middle, gain_mlp.astype(jnp.float32), offset_mlp.astype(jnp.float32)
    )
    d_middle_part, d_gain_mlp, d_offset_mlp = norm_back_two(d_normed_two)
    d_middle = grad_out + d_middle_part
    scaled_mid = BRANCH_SCALE * d_middle
    d_out_bias = jnp.sum(scaled_mid, axis=0)
    d_attn_full = lax.all_gather(scaled_mid.astype(jnp.bfloat16), "tensor", axis=0, tiled=True)
    d_out_w = contract_rows(attended, d_attn_full)
    d_attended = contract_cols(d_attn_full, out_weight).astype(jnp.bfloat16)

    def backward_block(carry, inputs):
        d_keys_acc, d_values_acc = carry
        row_start, logsum = inputs
        visible = visible_mask(seg_row, row_start, block_rows)
        query_block = lax.dynamic_slice_in_dim(queries, row_start, block_rows, 0)
        grad_block = lax.dynamic_slice_in_dim(d_attended, row_start, block_rows, 0)
        dq_pieces = []
        dk_pieces = []
        dv_pieces = []
        for head_index in range(heads_here):
            low_col = head_index * HEAD_DIM
            high_col = low_col + HEAD_DIM
            query_head = query_block[:, low_col:high_col]
            key_head = keys_all[:, low_col:high_col]
            grad_head = grad_block[:, low_col:high_col]
            raw_scores = contract_cols(query_head, key_head)
            scores = jnp.where(visible, raw_scores * score_scale, MASKED_SCORE)
            soft_weights = jnp.exp(scores - logsum[head_index][:, None])
            d_soft = contract_cols(grad_head, values_all[:, low_col:high_col])
            d_scores = soft_weights * (
                d_soft - jnp.sum(soft_weights * d_soft, axis=1, keepdims=True)
            )
            d_raw = (d_scores * score_scale).astype(jnp.bfloat16)
            dq_pieces.append(jnp.dot(d_raw, key_head, preferred_element_type=jnp.float32))
            dk_pieces.append(contract_rows(d_raw, query_head))
            dv_pieces.append(contract_rows(soft_weights.astype(jnp.bfloat16), grad_head))
        new_carry = (
            d_keys_acc + jnp.concatenate(dk_pieces, axis=1),
            d_values_acc + jnp.concatenate(dv_pieces, axis=1),
        )
        return (new_carry, jnp.concatenate(dq_pieces, axis=1))

    zero_acc = jnp.zeros((seq_len, local_cols), jnp.float32)
    (d_keys, d_values), dq_blocks = lax.scan(
        backward_block, (zero_acc, zero_acc), (starts, logsum_blocks)
    )
    d_queries = dq_blocks.reshape(seq_len, local_cols)
    d_projected = jnp.stack([d_queries, d_keys, d_values], axis=1).astype(jnp.bfloat16)
    part_sums = jnp.sum(d_projected, axis=0, dtype=jnp.float32)
    d_qv_bias = lax.dynamic_update_slice(
        jnp.zeros((2, model_width), jnp.float32),
        jnp.stack([part_sums[0], part_sums[2]]),
        (0, tensor_pos * local_cols),
    )
    d_flat = d_projected.reshape(seq_len, 3 * local_cols)
    d_qkv_w = contract_rows(full_one, d_flat).reshape(model_width, 3, local_cols)
    d_normed_one = lax.psum_scatter(
        contract_cols(d_flat, qkv_flat_weight).astype(jnp.bfloat16),
        "tensor",
        scatter_dimension=0,
        tiled=True,
    ).astype(jnp.float32)
    unused_one, norm_back_one = jax.vjp(
        layer_norm, residual_in, gain_attn.astype(jnp.float32), offset_attn.astype(jnp.float32)
    )
    d_input_part, d_gain_attn, d_offset_attn = norm_back_one(d_normed_one)
    grad_tokens = (d_middle + d_input_part).astype(jnp.bfloat16)
    d_fc_bias_full = lax.dynamic_update_slice(
        jnp.zeros((fc_bias_all.shape[0],), jnp.float32), d_fc_bias, (tensor_pos * hidden_cols,)
    )
    (
        sum_gain_attn,
        sum_offset_attn,
        sum_qv_bias,
        sum_out_bias,
        sum_gain_mlp,
        sum_offset_mlp,
        sum_fc_bias,
        sum_proj_bias,
    ) = (
        lax.psum(d_gain_attn.astype(jnp.bfloat16), "tensor").astype(jnp.float32),
        lax.psum(d_offset_attn.astype(jnp.bfloat16), "tensor").astype(jnp.float32),
        lax.psum(d_qv_bias.astype(jnp.bfloat16), "tensor").astype(jnp.float32),
        lax.psum(d_out_bias.astype(jnp.bfloat16), "tensor").astype(jnp.float32),
        lax.psum(d_gain_mlp.astype(jnp.bfloat16), "tensor").astype(jnp.float32),
        lax.psum(d_offset_mlp.astype(jnp.bfloat16), "tensor").astype(jnp.float32),
        lax.psum(d_fc_bias_full.astype(jnp.bfloat16), "tensor").astype(jnp.float32),
        lax.psum(d_proj_bias.astype(jnp.bfloat16), "tensor").astype(jnp.float32),
    )
    (
        grad_w_qkv,
        grad_w_attn_out,
        grad_ln1_gain,
        grad_ln1_bias,
        grad_b_qv,
        grad_b_attn_out,
        grad_ln2_gain,
        grad_ln2_bias,
        grad_b_fc,
        grad_b_proj,
    ) = (
        lax.psum_scatter(d_qkv_w, "dp", scatter_dimension=0, tiled=True),
        lax.psum_scatter(d_out_w, "dp", scatter_dimension=1, tiled=True),
        lax.psum_scatter(sum_gain_attn, "dp", scatter_dimension=0, tiled=True),
        lax.psum_scatter(sum_offset_attn, "dp", scatter_dimension=0, tiled=True),
        lax.psum_scatter(sum_qv_bias, "dp", scatter_dimension=1, tiled=True),
        lax.psum_scatter(sum_out_bias, "dp", scatter_dimension=0, tiled=True),
        lax.psum_scatter(sum_gain_mlp, "dp", scatter_dimension=0, tiled=True),
        lax.psum_scatter(sum_offset_mlp, "dp", scatter_dimension=0, tiled=True),
        lax.psum_scatter(sum_fc_bias, "dp", scatter_dimension=0, tiled=True),
        lax.psum_scatter(sum_proj_bias, "dp", scatter_dimension=0, tiled=True),
    )
    return (
        block_out,
        grad_tokens,
        grad_ln1_gain,
        grad_ln1_bias,
        grad_w_qkv,
        grad_b_qv,
        grad_w_attn_out,
        grad_b_attn_out,
        grad_ln2_gain,
        grad_ln2_bias,
        grad_w_fc,
        grad_b_fc,
        grad_w_proj,
        grad_b_proj,
    )


def solution(mesh):
    in_specs = (
        P(("dp", "tensor"), None),
        P("dp", None),
        P("dp"),
        P("dp"),
        P("dp", None, "tensor"),
        P(None, "dp"),
        P("tensor", "dp"),
        P("dp"),
        P("dp"),
        P("dp"),
        P("dp", "tensor"),
        P("dp"),
        P("tensor", "dp"),
        P("dp"),
        P(("dp", "tensor"), None),
    )
    out_specs = (
        P(("dp", "tensor"), None),
        P(("dp", "tensor"), None),
        P("dp"),
        P("dp"),
        P("dp", None, "tensor"),
        P(None, "dp"),
        P("tensor", "dp"),
        P("dp"),
        P("dp"),
        P("dp"),
        P("dp", "tensor"),
        P("dp"),
        P("tensor", "dp"),
        P("dp"),
    )
    return jax.shard_map(
        on_device, mesh=mesh, in_specs=in_specs, out_specs=out_specs, check_vma=False
    )
```

profile of v0, /device:TPU:0, one launch (start us, length us, event | category | flops | bytes accessed | tf_op | source)
XLA Modules:
  0.0 1494.2 jit_solution(269349831955712147)
XLA Ops:
  16.5 63.2 %all-reduce.15 = (bf16[768]{0:T(1024)(128)(2,1)}, bf16[768]{0:T(1024)(128)(2,1)}, bf16[768]{0:T(1024)(128)(2,1)}, bf16[768]{0:T(1024)(128)(2,1)S(1)}, bf16[768]{...) all-reduce(bf16[768]{0:T(1024)(128)(2,1)S(1)} %dynamic-update-slice, ...), channel_id=1, replica_groups=mesh['dp'=16,'tensor'=2] {'dp'}, use_global_device_ids=true, to_apply=%add.4 | all-reduce | flops 7680 | bytes 30720
  86.6 17.0 %all-gather = bf16[16,48,2]{1,2,0:T(2,128)(2,1)S(1)} all-gather(bf16[1,48,2]{1,2,0:T(2,128)(2,1)S(1)} %bitcast.226), channel_id=1, replica_groups=mesh['dp'=16,'tensor'=2] {'dp'}, dimensions={0}, use_global_device_ids=true | all-gather | bytes 3264 | tf_op jit(solution)/shard_map/all_gather | solution.py:72
  104.4 22.1 %all_gather.60 = bf16[384,768]{0,1:T(8,128)(2,1)} all-gather(bf16[384,48]{0,1:T(8,128)(2,1)S(1)} %copy-done.41), channel_id=1, replica_groups=mesh['dp'=16,'tensor'=2] {'dp'}, dimensions={1}, use_global_device_ids=true | all-gather | bytes 626688 | tf_op jit(solution)/shard_map/all_gather | solution.py:73
  129.1 7.4 add_convert_fusion
  138.2 145.9 %while.43 = (s32[]{:T(128)}, bf16[4,512,384]{2,1,0:T(8,128)(2,1)}, f32[4,6,512]{2,1,0:T(8,128)}, s32[4]{0:T(128)}, s32[2048]{0:T(1024)}, /*index=5*/s32[1,2048]{...) while((s32[]{:T(128)}, bf16[4,512,384]{2,1,0:T(8,128)(2,1)}, ...), condition=%wide.region_15.16_spmd, body=%wide.region_2.15_spmd.sunk | while | flops 1680012800 | bytes 86346096 | solution.py:124
  293.8 39.7 %reduce-scatter.12.cloned.1.call-done = bf16[1024,768]{1,0:T(8,128)(2,1)} async-done(((bf16[2048,768]{1,0:T(8,128)(2,1)}), bf16[1024,768]{1,0:T(8,128)(2,1)}) %reduce-scatter.12.cloned.1.call-update) | async-done | bytes 1572880 | tf_op jit(solution)/shard_map/reduce_scatter | solution.py:126
  340.2 38.0 %all-gather.17.cloned.1.call-done = bf16[1536,768]{0,1:T(8,128)(2,1)} async-done(((bf16[1536,48]{0,1:T(8,128)(2,1)}), bf16[1536,768]{0,1:T(8,128)(2,1)}) %all-gather.17.cloned.1.call-update) | async-done | bytes 2359312 | tf_op jit(solution)/shard_map/all_gather | solution.py:142
  381.0 42.4 %all-gather.19.cloned.1.call-done = bf16[2048,768]{1,0:T(8,128)(2,1)} async-done(((bf16[1024,768]{1,0:T(8,128)(2,1)}), bf16[2048,768]{1,0:T(8,128)(2,1)}) %all-gather.19.cloned.1.call-update) | async-done | bytes 3145744 | tf_op jit(solution)/shard_map/all_gather | solution.py:191
  423.4 44.7 %all-gather.15.cloned.1.call-done = bf16[768,1536]{1,0:T(8,128)(2,1)} async-done(((bf16[48,1536]{1,0:T(8,128)(2,1)}), bf16[768,1536]{1,0:T(8,128)(2,1)}) %all-gather.15.cloned.1.call-update) | async-done | bytes 2359312 | tf_op jit(solution)/shard_map/all_gather | solution.py:140
  468.2 45.9 %all-gather.13.cloned.1.call-done = bf16[2048,768]{1,0:T(8,128)(2,1)} async-done(((bf16[1024,768]{1,0:T(8,128)(2,1)}), bf16[2048,768]{1,0:T(8,128)(2,1)}) %all-gather.13.cloned.1.call-update) | async-done | bytes 3145744 | tf_op jit(solution)/shard_map/all_gather | solution.py:151
  514.1 47.8 %while.44 = (s32[]{:T(128)}, bf16[2,1024,1536]{2,1,0:T(8,128)(2,1)}, bf16[2,1024,1536]{2,1,0:T(8,128)(2,1)}, f32[2,1536]{1,0:T(2,128)S(1)}, s32[2]{0:T(128)S(1)}...) while((s32[]{:T(128)}, ...), condition=%wide.region_22.23_spmd, body=%wide.region_20.22_spmd.sunk | while | flops 4882168320 | bytes 102281512 | solution.py:203
  516.6 7.7 bitcast_dynamic-update-slice_fusion.7
  524.4 7.8 bitcast_dynamic-update-slice_fusion.8
  540.6 7.7 bitcast_dynamic-update-slice_fusion.7
  548.3 7.8 bitcast_dynamic-update-slice_fusion.8
  562.0 9.1 convolution_convert_fusion.1
  572.7 14.0 convolution_convert_fusion.2
  586.8 27.8 %reduce-scatter.16.cloned.1.call-done = bf16[1024,768]{1,0:T(8,128)(2,1)} async-done(((bf16[2048,768]{1,0:T(8,128)(2,1)}), bf16[1024,768]{1,0:T(8,128)(2,1)}) %reduce-scatter.16.cloned.1.call-update) | async-done | bytes 1572880 | tf_op jit(solution)/shard_map/reduce_scatter | solution.py:215
  618.6 41.6 %reduce-scatter.14.cloned.1.call-done = bf16[1024,768]{1,0:T(8,128)(2,1)} async-done(((bf16[2048,768]{1,0:T(8,128)(2,1)}), bf16[1024,768]{1,0:T(8,128)(2,1)}) %reduce-scatter.14.cloned.1.call-update) | async-done | bytes 1572880 | tf_op jit(solution)/shard_map/reduce_scatter | solution.py:156
  668.3 45.0 %all-gather.21.cloned.1.call-done = bf16[2048,768]{1,0:T(8,128)(2,1)} async-done(((bf16[1024,768]{1,0:T(8,128)(2,1)}), bf16[2048,768]{1,0:T(8,128)(2,1)}) %all-gather.21.cloned.1.call-update) | async-done | bytes 3145744 | tf_op jit(solution)/shard_map/all_gather | solution.py:230
  718.2 344.7 %while.45 = (s32[]{:T(128)}, f32[2048,384]{0,1:T(8,128)}, f32[2048,384]{0,1:T(8,128)}, bf16[4,512,384]{2,1,0:T(8,128)(2,1)}, s32[4]{0:T(128)}, /*index=5*/s32[20...) while((s32[]{:T(128)}, f32[2048,384]{0,1:T(8,128)}, ...), condition=%wide.region_33.34_spmd.clone, body=%wide.region_26.33_spmd.clone.sunk | while | flops 4111463936 | bytes 254159472 | solution.py:267
  1044.5 7.0 select_add_fusion.3
  1079.4 41.8 %reduce-scatter.18.cloned.1.call-done = bf16[1024,768]{1,0:T(8,128)(2,1)} async-done(((bf16[2048,768]{1,0:T(8,128)(2,1)}), bf16[1024,768]{1,0:T(8,128)(2,1)}) %reduce-scatter.18.cloned.1.call-update) | async-done | bytes 1572880 | tf_op jit(solution)/shard_map/reduce_scatter | solution.py:280
  1130.4 7.1 all-reduce.16
  1138.5 10.1 fusion.173
  1150.5 9.5 fusion.172
  1173.3 8.4 fusion.135
  1183.0 60.1 %all-reduce.14 = (f32[768]{0:T(1024)S(1)}, f32[768]{0:T(1024)S(1)}, f32[768]{0:T(1024)S(1)}, f32[768]{0:T(1024)S(1)}, f32[768]{0:T(1024)S(1)}, /*index=5*/f32[3072]{0:T(1024)S(1)}, f32[768]{0:T(1024)S(1)}) all-reduce(bf16[768]{0:T(1024)(128)(2,1)S(1)} %get-tuple-element.392, ...), channel_id=6, replica_groups=mesh['dp'=16,'tensor'=2] {'dp'}, use_global_device_ids=true, to_apply=%region_39.40.clone | all-reduce | flops 7680 | bytes 46080
  1248.6 26.4 %reduce-scatter.26.cloned.1.call-done = f32[1536,48]{0,1:T(8,128)} async-done(((f32[1536,768]{0,1:T(8,128)}), f32[1536,48]{0,1:T(8,128)}) %reduce-scatter.26.cloned.1.call-update) | async-done | bytes 294928 | tf_op jit(solution)/shard_map/reduce_scatter | solution.py:213
  1275.1 78.9 %reduce-scatter.24.cloned.1.call-done = f32[48,1536]{1,0:T(8,128)} async-done(((f32[768,1536]{1,0:T(8,128)}), f32[48,1536]{1,0:T(8,128)}) %reduce-scatter.24.cloned.1.call-update) | async-done | bytes 294928 | tf_op jit(solution)/shard_map/reduce_scatter | solution.py:212
  1353.9 61.6 %reduce-scatter.22.cloned.1.call-done = f32[384,48]{0,1:T(8,128)} async-done(((f32[384,768]{0,1:T(8,128)}), f32[384,48]{0,1:T(8,128)}) %reduce-scatter.22.cloned.1.call-update) | async-done | bytes 73744 | tf_op jit(solution)/shard_map/reduce_scatter | solution.py:326
  1415.5 71.9 %reduce-scatter.20.cloned.1.call-done = f32[48,3,384]{2,0,1:T(8,128)} async-done(((f32[768,3,384]{2,0,1:T(8,128)}), f32[48,3,384]{2,0,1:T(8,128)}) %reduce-scatter.20.cloned.1.call-update) | async-done | bytes 221200 | tf_op jit(solution)/shard_map/reduce_scatter | solution.py:325
  (563 shorter events, 575.9 us)
Async XLA Ops:
  7.2 77.5 %copy-start = (bf16[1024,768]{1,0:T(8,128)(2,1)S(1)}, bf16[1024,768]{1,0:T(8,128)(2,1)}, u32[]{:S(2)}) copy-start(bf16[1024,768]{1,0:T(8,128)(2,1)} %param.21) | copy-start | bytes 4718596
  7.2 119.3 %all-gather.11.cloned.1.call-start = ((), (), s32[]{:S(2)}) async-start(), calls=%async_computation.10 | async-start | bytes 1880064 | tf_op jit(solution)/shard_map/all_gather | solution.py:71
  7.9 121.2 %all-gather.9.cloned.1.call-start = ((), (), s32[]{:S(2)}) async-start(), calls=%async_computation.9 | async-start | bytes 4718592 | tf_op jit(solution)/shard_map/all_gather | solution.py:85
  86.5 246.9 %reduce-scatter.12.cloned.1.call-start = ((), (), s32[]{:S(2)}) async-start(), calls=%async_computation.11 | async-start | bytes 4718592 | tf_op jit(solution)/shard_map/reduce_scatter | solution.py:126
  290.3 43.2 %copy-start.1 = (bf16[1024,768]{1,0:T(8,128)(2,1)S(1)}, bf16[1024,768]{1,0:T(8,128)(2,1)}, u32[]{:S(2)}) copy-start(bf16[1024,768]{1,0:T(8,128)(2,1)} %param.21) | copy-start | bytes 4718596
  290.3 87.9 %all-gather.17.cloned.1.call-start = ((), (), s32[]{:S(2)}) async-start(), calls=%async_computation.14 | async-start | bytes 2506752 | tf_op jit(solution)/shard_map/all_gather | solution.py:142
  290.9 132.5 %all-gather.19.cloned.1.call-start = ((), (), s32[]{:S(2)}) async-start(), calls=%async_computation.16 | async-start | bytes 4718592 | tf_op jit(solution)/shard_map/all_gather | solution.py:191
  293.1 175.1 %all-gather.15.cloned.1.call-start = ((), (), s32[]{:S(2)}) async-start(), calls=%async_computation.13 | async-start | bytes 2506752 | tf_op jit(solution)/shard_map/all_gather | solution.py:140
  293.7 220.4 %all-gather.13.cloned.1.call-start = ((), (), s32[]{:S(2)}) async-start(), calls=%async_computation.12 | async-start | bytes 4718592 | tf_op jit(solution)/shard_map/all_gather | solution.py:151
  293.7 43.5 %copy-start.23 = (f32[768]{0:T(1024)}, f32[768]{0:T(1024)S(1)}, u32[]{:S(2)}) copy-start(f32[768]{0:T(1024)S(1)} %convert_element_type.220) | copy-start | bytes 9220
  293.8 43.5 %copy-start.31 = (f32[768]{0:T(1024)}, f32[768]{0:T(1024)S(1)}, u32[]{:S(2)}) copy-start(f32[768]{0:T(1024)S(1)} %convert_element_type.221) | copy-start | bytes 9220
  340.0 274.6 %reduce-scatter.16.cloned.1.call-start = ((), (), s32[]{:S(2)}) async-start(), calls=%async_computation.17 | async-start | bytes 4718592 | tf_op jit(solution)/shard_map/reduce_scatter | solution.py:215
  571.1 89.1 %reduce-scatter.14.cloned.1.call-start = ((), (), s32[]{:S(2)}) async-start(), calls=%async_computation.15 | async-start | bytes 4718592 | tf_op jit(solution)/shard_map/reduce_scatter | solution.py:156
  572.7 41.9 %copy-start.32 = (f32[768]{0:T(1024)S(1)}, f32[768]{0:T(1024)}, u32[]{:S(2)}) copy-start(f32[768]{0:T(1024)} %copy-done.31) | copy-start | bytes 9220
  572.7 41.9 %copy-start.34 = (f32[1024]{0:T(1024)S(1)}, f32[1024]{0:T(1024)}, u32[]{:S(2)}) copy-start(f32[1024]{0:T(1024)} %copy-done.33) | copy-start | bytes 12292
  586.7 27.9 %copy-start.24 = (f32[768]{0:T(1024)S(1)}, f32[768]{0:T(1024)}, u32[]{:S(2)}) copy-start(f32[768]{0:T(1024)} %copy-done.23) | copy-start | bytes 9220
  586.7 27.9 %copy-start.28 = (f32[1024]{0:T(1024)S(1)}, f32[1024]{0:T(1024)}, u32[]{:S(2)}) copy-start(f32[1024]{0:T(1024)} %copy-done.27) | copy-start | bytes 12292
  586.7 31.8 %copy-start.40 = (f32[1024]{0:T(1024)S(1)}, f32[1024]{0:T(1024)}, u32[]{:S(2)}) copy-start(f32[1024]{0:T(1024)} %copy-done.39) | copy-start | bytes 12292
  586.8 126.5 %all-gather.21.cloned.1.call-start = ((), (), s32[]{:S(2)}) async-start(), calls=%async_computation.18 | async-start | bytes 4718592 | tf_op jit(solution)/shard_map/all_gather | solution.py:230
  668.2 453.0 %reduce-scatter.18.cloned.1.call-start = ((), (), s32[]{:S(2)}) async-start(), calls=%async_computation.19 | async-start | bytes 4718592 | tf_op jit(solution)/shard_map/reduce_scatter | solution.py:280
  668.2 50.0 %copy-start.5 = (bf16[2048,384]{1,0:T(8,128)(2,1)S(1)}, bf16[2048,384]{1,0:T(8,128)(2,1)}, u32[]{:S(2)}) copy-start(bf16[2048,384]{1,0:T(8,128)(2,1)} %copy-done.4) | copy-start | bytes 4718596
  668.2 50.0 %copy-start.7 = (bf16[2048,384]{1,0:T(8,128)(2,1)S(1)}, bf16[2048,384]{1,0:T(8,128)(2,1)}, u32[]{:S(2)}) copy-start(bf16[2048,384]{1,0:T(8,128)(2,1)} %copy-done.6) | copy-start | bytes 4718596
  1077.7 43.5 %copy-start.3 = (bf16[1024,768]{1,0:T(8,128)(2,1)S(1)}, bf16[1024,768]{1,0:T(8,128)(2,1)}, u32[]{:S(2)}) copy-start(bf16[1024,768]{1,0:T(8,128)(2,1)} %param.21) | copy-start | bytes 4718596
  1077.7 43.5 %copy-start.22 = (f32[1024]{0:T(1024)S(1)}, f32[1024]{0:T(1024)}, u32[]{:S(2)}) copy-start(f32[1024]{0:T(1024)} %copy-done.21) | copy-start | bytes 12292
  1077.7 43.5 %copy-start.26 = (f32[768]{0:T(1024)S(1)}, f32[768]{0:T(1024)}, u32[]{:S(2)}) copy-start(f32[768]{0:T(1024)} %copy-done.25) | copy-start | bytes 9220
  1077.7 45.9 %copy-start.38 = (f32[1024]{0:T(1024)S(1)}, f32[1024]{0:T(1024)}, u32[]{:S(2)}) copy-start(f32[1024]{0:T(1024)} %copy-done.37) | copy-start | bytes 12292
  1077.7 45.9 %copy-start.30 = (f32[1024]{0:T(1024)S(1)}, f32[1024]{0:T(1024)}, u32[]{:S(2)}) copy-start(f32[1024]{0:T(1024)} %copy-done.29) | copy-start | bytes 12292
  1077.7 169.5 %reduce-scatter.28.cloned.1.call-start = ((), (), s32[]{:S(2)}) async-start(), calls=%async_computation.24 | async-start | bytes 417792
  1138.5 136.6 %reduce-scatter.26.cloned.1.call-start = ((), (), s32[]{:S(2)}) async-start(), calls=%async_computation.23 | async-start | bytes 5013504 | tf_op jit(solution)/shard_map/reduce_scatter | solution.py:213
  1148.6 205.3 %reduce-scatter.24.cloned.1.call-start = ((), (), s32[]{:S(2)}) async-start(), calls=%async_computation.22 | async-start | bytes 5013504 | tf_op jit(solution)/shard_map/reduce_scatter | solution.py:212
  1160.0 255.5 %reduce-scatter.22.cloned.1.call-start = ((), (), s32[]{:S(2)}) async-start(), calls=%async_computation.21 | async-start | bytes 1253376 | tf_op jit(solution)/shard_map/reduce_scatter | solution.py:326
  1166.3 321.1 %reduce-scatter.20.cloned.1.call-start = ((), (), s32[]{:S(2)}) async-start(), calls=%async_computation.20 | async-start | bytes 3760128 | tf_op jit(solution)/shard_map/reduce_scatter | solution.py:325
  (53 other events, 246.3 us)
Sparse Core Ops, SparseCore 0:
  10.3 43.2 all-gather.10
  86.6 42.1 all-gather.8
  290.4 43.0 reduce-scatter.11
  335.8 42.3 all-gather.16
  379.7 43.7 all-gather.18
  425.8 42.3 all-gather.14
  470.3 43.7 all-gather.12
  571.2 43.3 reduce-scatter.15
  616.8 43.3 reduce-scatter.13
  668.3 44.9 all-gather.20
  1077.8 43.3 reduce-scatter.17
  1138.6 56.7 reduce-scatter.27
  1200.3 74.7 reduce-scatter.25
  1279.4 74.5 reduce-scatter.23
  1358.4 57.0 reduce-scatter.21
  1420.3 67.0 reduce-scatter.19
where the time goes:
time: 1500 us; the launch traced here: 1490 us
  waiting for transfers between devices  608 us (41%)
  matrix products  437 us (29%)
  blocking collectives  169 us (11%)
  other arithmetic  126 us (8%)
  local copies, waits for them, and re-layouts  107 us (7%)
  loops' own time  29.1 us (2%)
  between operations  17.5 us (1%)
    dot_general x77, matrix products, contract_cols(): lax.dot_general(left, right, (((1,), (1,)), ((), ())), preferred_element_...  205 us
    dot_general x52, matrix products, contract_rows(): lax.dot_general(left, right, (((0,), (0,)), ((), ())), preferred_element_...  126 us
    unnamed x2, blocking collectives  123 us
    reduce_scatter x1, waiting for transfers between devices, on_device(): lax.psum_scatter(d_fc_w, 'dp', scatter_dimension=0, tiled=True)  78.9 us
    reduce_scatter x1, waiting for transfers between devices, on_device(): lax.psum_scatter(d_qkv_w, 'dp', scatter_dimension=0, tiled=True)  71.9 us
    reduce_scatter x1, waiting for transfers between devices, on_device(): lax.psum_scatter(d_out_w, 'dp', scatter_dimension=1, tiled=True)  61.6 us
    all_gather x1, waiting for transfers between devices, on_device(): full_two = lax.all_gather(normed_two, 'tensor', axis=0, tiled=True)  45.9 us
    all_gather x1, waiting for transfers between devices, on_device(): lax.all_gather(scaled_mid.astype(jnp.bfloat16), 'tensor', axis=0, tiled=T...  45 us
  transfers between devices with their start and end apart: 16, of which 13 were waited for; matrix products, arithmetic and copies ran while one was open for 6% of the time, Pallas kernels for 0%

commit v1 on v0

--- a/solution.py
+++ b/solution.py
@@ -7,6 +7,19 @@
 EPSILON = 1e-05
 BRANCH_SCALE = 48.0 ** (-0.5)
 MASKED_SCORE = -1e30
+
+
+def ring_gather(value, axis, dim):
+    size, index, extent = (lax.axis_size(axis), lax.axis_index(axis), value.shape[dim])
+    upward = [(i, (i + 1) % size) for i in range(size)]
+    whole = jnp.zeros((*value.shape[:dim], size * extent, *value.shape[dim + 1 :]), value.dtype)
+    held = value
+    for step in range(size):
+        owner = (index - step) % size
+        whole = lax.dynamic_update_slice_in_dim(whole, held, owner * extent, axis=dim)
+        if step < size - 1:
+            held = lax.ppermute(held, axis, upward)
+    return whole
 
 
 def layer_norm(values, gain, offsets):
@@ -139,7 +152,7 @@
         lax.all_gather(ln2_bias, "dp", axis=0, tiled=True),
         lax.all_gather(w_fc, "dp", axis=0, tiled=True),
         lax.all_gather(b_fc, "dp", axis=0, tiled=True),
-        lax.all_gather(w_proj, "dp", axis=1, tiled=True),
+        ring_gather(w_proj, "dp", 1),
         lax.all_gather(b_proj, "dp", axis=0, tiled=True),
     )
     fc_bias = lax.dynamic_slice_in_dim(

time: 1500 us -> 1570 us (1.047)
  waiting for transfers between devices: 608 us -> 645 us
  loops' own time: 29.1 us -> 47.9 us
    ppermute x0 -> x15, waiting for transfers between devices: none -> 105 us  [ring_gather(): held = lax.ppermute(held, axis, upward)]
    all_gather x1, waiting for transfers between devices: 38 us -> 7.11 us  [on_device(): lax.all_gather(w_proj, 'dp', axis=1, tiled=True)]
    reduce_scatter x1, waiting for transfers between devices: 27.8 us -> 0.02 us  [on_device(): lax.psum_scatter(contract_cols(lax.slice_in_dim(d_pre_all, 0, lax.axis_si...]
    another operation x1, loops' own time: 16.5 us -> 35.3 us  [on_device(): lax.scan(backward_block, (zero_acc, zero_acc), (starts, logsum_blocks))]
  transfers between devices with their start and end apart: 16 -> 31, of which waited for: 13 -> 26; matrix products, arithmetic and copies ran while one was open for 6% -> 9% of each run, Pallas kernels for 0% -> 0%
where the time goes in v1:
time: 1570 us; the launch traced here: 1560 us
  waiting for transfers between devices  645 us (41%)
  matrix products  437 us (28%)
  blocking collectives  169 us (11%)
  other arithmetic  126 us (8%)
  local copies, waits for them, and re-layouts  112 us (7%)
  loops' own time  47.9 us (3%)
  between operations  18.1 us (1%)
    dot_general x77, matrix products, contract_cols(): lax.dot_general(left, right, (((1,), (1,)), ((), ())), preferred_element_...  205 us
    dot_general x52, matrix products, contract_rows(): lax.dot_general(left, right, (((0,), (0,)), ((), ())), preferred_element_...  126 us
    unnamed x2, blocking collectives  123 us
    ppermute x15, waiting for transfers between devices, ring_gather(): held = lax.ppermute(held, axis, upward)  105 us
    reduce_scatter x1, waiting for transfers between devices, on_device(): lax.psum_scatter(d_fc_w, 'dp', scatter_dimension=0, tiled=True)  79 us
    reduce_scatter x1, waiting for transfers between devices, on_device(): lax.psum_scatter(d_qkv_w, 'dp', scatter_dimension=0, tiled=True)  71.9 us
    reduce_scatter x1, waiting for transfers between devices, on_device(): lax.psum_scatter(d_out_w, 'dp', scatter_dimension=1, tiled=True)  61.6 us
    all_gather x1, waiting for transfers between devices, on_device(): full_two = lax.all_gather(normed_two, 'tensor', axis=0, tiled=True)  45.9 us
  transfers between devices with their start and end apart: 31, of which 26 were waited for; matrix products, arithmetic and copies ran while one was open for 9% of the time, Pallas kernels for 0%

profile of v1, /device:TPU:0, one launch (start us, length us, event | category | flops | bytes accessed | tf_op | source)
XLA Modules:
  0.0 1555.7 jit_solution(7905600409455726261)
XLA Ops:
  16.5 63.2 %all-reduce.15 = (bf16[768]{0:T(1024)(128)(2,1)}, bf16[768]{0:T(1024)(128)(2,1)}, bf16[768]{0:T(1024)(128)(2,1)}, bf16[768]{0:T(1024)(128)(2,1)S(1)}, bf16[768]{...) all-reduce(bf16[768]{0:T(1024)(128)(2,1)S(1)} %dynamic-update-slice, ...), channel_id=1, replica_groups=mesh['dp'=16,'tensor'=2] {'dp'}, use_global_device_ids=true, to_apply=%add.4 | all-reduce | flops 7680 | bytes 30720
  86.6 17.0 %all-gather = bf16[16,48,2]{1,2,0:T(2,128)(2,1)S(1)} all-gather(bf16[1,48,2]{1,2,0:T(2,128)(2,1)S(1)} %bitcast.226), channel_id=1, replica_groups=mesh['dp'=16,'tensor'=2] {'dp'}, dimensions={0}, use_global_device_ids=true | all-gather | bytes 3264 | tf_op jit(solution)/shard_map/all_gather | solution.py:85
  104.4 22.1 %all_gather.59 = bf16[384,768]{0,1:T(8,128)(2,1)} all-gather(bf16[384,48]{0,1:T(8,128)(2,1)S(1)} %copy-done.44), channel_id=1, replica_groups=mesh['dp'=16,'tensor'=2] {'dp'}, dimensions={1}, use_global_device_ids=true | all-gather | bytes 626688 | tf_op jit(solution)/shard_map/all_gather | solution.py:86
  129.1 7.4 add_convert_fusion
  138.1 145.7 %while.43 = (s32[]{:T(128)}, bf16[4,512,384]{2,1,0:T(8,128)(2,1)}, f32[4,6,512]{2,1,0:T(8,128)}, s32[4]{0:T(128)}, s32[2048]{0:T(1024)}, /*index=5*/s32[1,2048]{...) while((s32[]{:T(128)}, bf16[4,512,384]{2,1,0:T(8,128)(2,1)}, ...), condition=%wide.region_15.16_spmd, body=%wide.region_2.15_spmd.sunk | while | flops 1680012800 | bytes 86346096 | solution.py:137
  293.6 39.6 %reduce-scatter.12.cloned.1.call-done = bf16[1024,768]{1,0:T(8,128)(2,1)} async-done(((bf16[2048,768]{1,0:T(8,128)(2,1)}), bf16[1024,768]{1,0:T(8,128)(2,1)}) %reduce-scatter.12.cloned.1.call-update) | async-done | bytes 1572880 | tf_op jit(solution)/shard_map/reduce_scatter | solution.py:139
  346.7 8.7 collective-permute-done.1
  355.4 7.2 collective-permute-done.2
  362.6 10.4 collective-permute-done.3
  384.4 41.2 %all-gather.17.cloned.1.call-done = bf16[2048,768]{1,0:T(8,128)(2,1)} async-done(((bf16[1024,768]{1,0:T(8,128)(2,1)}), bf16[2048,768]{1,0:T(8,128)(2,1)}) %all-gather.17.cloned.1.call-update) | async-done | bytes 3145744 | tf_op jit(solution)/shard_map/all_gather | solution.py:204
  425.6 44.7 %all-gather.15.cloned.1.call-done = bf16[768,1536]{1,0:T(8,128)(2,1)} async-done(((bf16[48,1536]{1,0:T(8,128)(2,1)}), bf16[768,1536]{1,0:T(8,128)(2,1)}) %all-gather.15.cloned.1.call-update) | async-done | bytes 2359312 | tf_op jit(solution)/shard_map/all_gather | solution.py:153
  470.4 45.9 %all-gather.13.cloned.1.call-done = bf16[2048,768]{1,0:T(8,128)(2,1)} async-done(((bf16[1024,768]{1,0:T(8,128)(2,1)}), bf16[2048,768]{1,0:T(8,128)(2,1)}) %all-gather.13.cloned.1.call-update) | async-done | bytes 3145744 | tf_op jit(solution)/shard_map/all_gather | solution.py:164
  516.3 47.9 %while.44 = (s32[]{:T(128)}, bf16[2,1024,1536]{2,1,0:T(8,128)(2,1)}, bf16[2,1024,1536]{2,1,0:T(8,128)(2,1)}, f32[2,1536]{1,0:T(2,128)S(1)}, s32[2]{0:T(128)S(1)}...) while((s32[]{:T(128)}, ...), condition=%wide.region_22.23_spmd, body=%wide.region_20.22_spmd.sunk | while | flops 4882168320 | bytes 111718728 | solution.py:216
  518.9 7.7 bitcast_dynamic-update-slice_fusion.7
  526.6 7.8 bitcast_dynamic-update-slice_fusion.8
  542.8 7.7 bitcast_dynamic-update-slice_fusion.7
  550.5 7.8 bitcast_dynamic-update-slice_fusion.8
  564.3 9.0 convolution_convert_fusion.1
  590.7 7.2 collective-permute-done.7
  648.9 14.2 convolution_convert_fusion.2
  668.9 33.7 %reduce-scatter.14.cloned.1.call-done = bf16[1024,768]{1,0:T(8,128)(2,1)} async-done(((bf16[2048,768]{1,0:T(8,128)(2,1)}), bf16[1024,768]{1,0:T(8,128)(2,1)}) %reduce-scatter.14.cloned.1.call-update) | async-done | bytes 1572880 | tf_op jit(solution)/shard_map/reduce_scatter | solution.py:169
  710.7 45.0 %all-gather.21.cloned.1.call-done = bf16[2048,768]{1,0:T(8,128)(2,1)} async-done(((bf16[1024,768]{1,0:T(8,128)(2,1)}), bf16[2048,768]{1,0:T(8,128)(2,1)}) %all-gather.21.cloned.1.call-update) | async-done | bytes 3145744 | tf_op jit(solution)/shard_map/all_gather | solution.py:243
  760.7 363.6 %while.45 = (s32[]{:T(128)}, f32[2048,384]{0,1:T(8,128)}, f32[2048,384]{0,1:T(8,128)}, bf16[4,512,384]{2,1,0:T(8,128)(2,1)}, s32[4]{0:T(128)}, /*index=5*/s32[20...) while((s32[]{:T(128)}, f32[2048,384]{0,1:T(8,128)}, ...), condition=%wide.region_33.34_spmd.clone, body=%wide.region_26.33_spmd.clone.sunk | while | flops 4111463936 | bytes 254159472 | solution.py:280
  1140.8 41.8 %reduce-scatter.18.cloned.1.call-done = bf16[1024,768]{1,0:T(8,128)(2,1)} async-done(((bf16[2048,768]{1,0:T(8,128)(2,1)}), bf16[1024,768]{1,0:T(8,128)(2,1)}) %reduce-scatter.18.cloned.1.call-update) | async-done | bytes 1572880 | tf_op jit(solution)/shard_map/reduce_scatter | solution.py:293
  1199.9 10.0 fusion.173
  1211.9 9.6 fusion.172
  1234.7 8.5 fusion.135
  1244.4 60.0 %all-reduce.14 = (f32[768]{0:T(1024)S(1)}, f32[768]{0:T(1024)S(1)}, f32[768]{0:T(1024)S(1)}, f32[768]{0:T(1024)S(1)}, f32[768]{0:T(1024)S(1)}, /*index=5*/f32[3072]{0:T(1024)S(1)}, f32[768]{0:T(1024)S(1)}) all-reduce(bf16[768]{0:T(1024)(128)(2,1)S(1)} %get-tuple-element.392, ...), channel_id=6, replica_groups=mesh['dp'=16,'tensor'=2] {'dp'}, use_global_device_ids=true, to_apply=%region_39.40.clone | all-reduce | flops 7680 | bytes 46080
  1310.0 26.5 %reduce-scatter.26.cloned.1.call-done = f32[1536,48]{0,1:T(8,128)} async-done(((f32[1536,768]{0,1:T(8,128)}), f32[1536,48]{0,1:T(8,128)}) %reduce-scatter.26.cloned.1.call-update) | async-done | bytes 294928 | tf_op jit(solution)/shard_map/reduce_scatter | solution.py:226
  1336.5 79.0 %reduce-scatter.24.cloned.1.call-done = f32[48,1536]{1,0:T(8,128)} async-done(((f32[768,1536]{1,0:T(8,128)}), f32[48,1536]{1,0:T(8,128)}) %reduce-scatter.24.cloned.1.call-update) | async-done | bytes 294928 | tf_op jit(solution)/shard_map/reduce_scatter | solution.py:225
  1415.4 61.6 %reduce-scatter.22.cloned.1.call-done = f32[384,48]{0,1:T(8,128)} async-done(((f32[384,768]{0,1:T(8,128)}), f32[384,48]{0,1:T(8,128)}) %reduce-scatter.22.cloned.1.call-update) | async-done | bytes 73744 | tf_op jit(solution)/shard_map/reduce_scatter | solution.py:339
  1477.1 71.9 %reduce-scatter.20.cloned.1.call-done = f32[48,3,384]{2,0,1:T(8,128)} async-done(((f32[768,3,384]{2,0,1:T(8,128)}), f32[48,3,384]{2,0,1:T(8,128)}) %reduce-scatter.20.cloned.1.call-update) | async-done | bytes 221200 | tf_op jit(solution)/shard_map/reduce_scatter | solution.py:338
  (618 shorter events, 673.0 us)
Async XLA Ops:
  7.2 119.3 %all-gather.11.cloned.1.call-start = ((), (), s32[]{:S(2)}) async-start(), calls=%async_computation.10 | async-start | bytes 1880064 | tf_op jit(solution)/shard_map/all_gather | solution.py:84
  7.9 121.2 %all-gather.9.cloned.1.call-start = ((), (), s32[]{:S(2)}) async-start(), calls=%async_computation.9 | async-start | bytes 4718592 | tf_op jit(solution)/shard_map/all_gather | solution.py:98
  86.5 246.7 %reduce-scatter.12.cloned.1.call-start = ((), (), s32[]{:S(2)}) async-start(), calls=%async_computation.11 | async-start | bytes 4718592 | tf_op jit(solution)/shard_map/reduce_scatter | solution.py:139
  290.0 90.1 %all-gather.19.cloned.1.call-start = ((), (), s32[]{:S(2)}) async-start(), calls=%async_computation.16 | async-start | bytes 2506752 | tf_op jit(solution)/shard_map/all_gather | solution.py:195
  290.6 135.0 %all-gather.17.cloned.1.call-start = ((), (), s32[]{:S(2)}) async-start(), calls=%async_computation.15 | async-start | bytes 4718592 | tf_op jit(solution)/shard_map/all_gather | solution.py:204
  292.9 177.5 %all-gather.15.cloned.1.call-start = ((), (), s32[]{:S(2)}) async-start(), calls=%async_computation.13 | async-start | bytes 2506752 | tf_op jit(solution)/shard_map/all_gather | solution.py:153
  293.4 222.9 %all-gather.13.cloned.1.call-start = ((), (), s32[]{:S(2)}) async-start(), calls=%async_computation.12 | async-start | bytes 4718592 | tf_op jit(solution)/shard_map/all_gather | solution.py:164
  339.2 324.0 %reduce-scatter.16.cloned.1.call-start = ((), (), s32[]{:S(2)}) async-start(), calls=%async_computation.17 | async-start | bytes 4718592 | tf_op jit(solution)/shard_map/reduce_scatter | solution.py:228
  339.3 7.4 collective-permute-start
  346.6 8.7 collective-permute-start.1
  355.3 7.3 collective-permute-start.2
  362.6 10.4 collective-permute-start.3
  362.6 153.7 %copy-start.19 = (bf16[1536,768]{0,1:T(8,128)(2,1)}, bf16[1536,768]{0,1:T(8,128)(2,1)S(1)}, u32[]{:S(2)}) copy-start(bf16[1536,768]{0,1:T(8,128)(2,1)S(1)} %constant_dynamic-update-slice_fusion.15) | copy-start | bytes 7077892
  373.0 202.9 %collective-permute-start.4 = (bf16[1536,48]{0,1:T(8,128)(2,1)}, bf16[1536,48]{0,1:T(8,128)(2,1)}, u32[]{:S(2)}, u32[]{:S(2)}) collective-permute-start(bf16[1536,48]{0,1:T(8,128)(2,1)} %collective-permute-done.3), channel_id=1, source_target_pairs={{0,2},{2,4},{4,6},{6,8},{8,10},{10,12},{12,14},{14,16},{16,18},{18... | collective-permute-start | bytes 442376 | tf_op jit(solution)/shard_map/ppermute | solution.py:21
  573.3 129.4 %reduce-scatter.14.cloned.1.call-start = ((), (), s32[]{:S(2)}) async-start(), calls=%async_computation.14 | async-start | bytes 4718592 | tf_op jit(solution)/shard_map/reduce_scatter | solution.py:169
  575.9 7.5 collective-permute-start.5
  583.4 7.3 collective-permute-start.6
  590.7 7.3 collective-permute-start.7
  598.0 7.3 collective-permute-start.8
  605.2 7.3 collective-permute-start.9
  612.5 7.3 collective-permute-start.10
  619.8 7.3 collective-permute-start.11
  627.0 7.3 collective-permute-start.12
  634.3 7.3 collective-permute-start.13
  641.6 7.3 collective-permute-start.14
  663.1 92.6 %all-gather.21.cloned.1.call-start = ((), (), s32[]{:S(2)}) async-start(), calls=%async_computation.18 | async-start | bytes 4718592 | tf_op jit(solution)/shard_map/all_gather | solution.py:243
  710.6 471.9 %reduce-scatter.18.cloned.1.call-start = ((), (), s32[]{:S(2)}) async-start(), calls=%async_computation.19 | async-start | bytes 4718592 | tf_op jit(solution)/shard_map/reduce_scatter | solution.py:293
  1139.1 169.5 %reduce-scatter.28.cloned.1.call-start = ((), (), s32[]{:S(2)}) async-start(), calls=%async_computation.24 | async-start | bytes 417792
  1199.9 136.6 %reduce-scatter.26.cloned.1.call-start = ((), (), s32[]{:S(2)}) async-start(), calls=%async_computation.23 | async-start | bytes 5013504 | tf_op jit(solution)/shard_map/reduce_scatter | solution.py:226
  1210.0 205.5 %reduce-scatter.24.cloned.1.call-start = ((), (), s32[]{:S(2)}) async-start(), calls=%async_computation.22 | async-start | bytes 5013504 | tf_op jit(solution)/shard_map/reduce_scatter | solution.py:225
  1221.4 255.7 %reduce-scatter.22.cloned.1.call-start = ((), (), s32[]{:S(2)}) async-start(), calls=%async_computation.21 | async-start | bytes 1253376 | tf_op jit(solution)/shard_map/reduce_scatter | solution.py:339
  1227.7 321.3 %reduce-scatter.20.cloned.1.call-start = ((), (), s32[]{:S(2)}) async-start(), calls=%async_computation.20 | async-start | bytes 3760128 | tf_op jit(solution)/shard_map/reduce_scatter | solution.py:338
  (72 other events, 782.2 us)
Sparse Core Ops, SparseCore 0:
  10.3 43.2 all-gather.10
  86.6 42.1 all-gather.8
  290.1 43.0 reduce-scatter.11
  335.6 44.4 all-gather.18
  381.6 44.0 all-gather.16
  428.0 42.3 all-gather.14
  472.6 43.7 all-gather.12
  573.4 43.3 reduce-scatter.15
  663.2 39.4 reduce-scatter.13
  710.7 44.9 all-gather.20
  1139.2 43.3 reduce-scatter.17
  1200.0 56.7 reduce-scatter.27
  1261.7 74.7 reduce-scatter.25
  1340.8 74.6 reduce-scatter.23
  1419.9 57.1 reduce-scatter.21
  1481.9 67.0 reduce-scatter.19
